TPU v7x, 32 devices: a whole 2x2x4 slice. The times are simulated.
32 devices in a mesh: amp: 4 (over y, core), own: 8 (over z, x).
Axes of the slice: x: 2, y: 2, z: 4, core: 2. Of those that a mesh axis runs over, the one named last changes fastest.
Arguments:
- amplitudes: bfloat16 [32, 2304, 192], P('own', None, 'amp'), may hold values from -6 to 6
- integrals: bfloat16 [32, 1152, 2304], P('own'), as said below
- occ_irrep: int32 [34], replicated, may hold values from 0 to 7, as said below
- tile_irrep: int32 [18], replicated, may hold values from 0 to 7, as said below
Outputs:
- cycle_term: bfloat16 [2304, 2304], P(('amp', 'own'))
Inputs may be any that keep to these rules, and one draw needn't show every extreme that they name: `occ_irrep`: labels of the D2h group, combined by XOR; every label occurs, and all labels occur equally often up to one. `tile_irrep`: labels of the D2h group, combined by XOR; every label occurs, and all labels occur equally often up to one, so some label has exactly 3 tiles. integrals[k, c, (j, b)] is zero unless the labels of k, c, j and b combine by XOR to 0.
All inputs are finite; a program needn't handle non-finite values.
Results may differ from a plain program's by a relative error of at most 0.001.
Values may be sent and summed in bfloat16 or wider, within the bound.
A program may use at most 128 MiB of HBM per device.

v0:
```python
import jax
import jax.numpy as jnp
from jax import lax
from jax.sharding import PartitionSpec as P

V = 1152
TILE = 64
NI = 2


def tile_ranks(tile_irrep):
    count = tile_irrep.shape[0]
    index = jnp.arange(count, dtype=jnp.int32)
    same = (tile_irrep[:, None] == tile_irrep[None, :]) & (index[None, :] < index[:, None])
    return jnp.sum(same.astype(jnp.int32), axis=1)


def shards(amplitudes, integrals, occ_irrep, tile_irrep):
    amp_index = lax.axis_index("amp")
    own_index = lax.axis_index("own")
    n_amp = lax.axis_size("amp")
    n_own = lax.axis_size("own")
    regrouped = lax.all_to_all(amplitudes, "amp", split_axis=1, concat_axis=2, tiled=True)
    k_local, rows, packed_width = regrouped.shape
    slot_count = packed_width // TILE
    virt_lab = jnp.repeat(tile_irrep, TILE)
    row_all = jnp.bitwise_xor(jnp.repeat(occ_irrep[:NI], V), jnp.tile(virt_lab, NI))
    row_lab = lax.dynamic_slice_in_dim(row_all, amp_index * rows, rows)
    k_lab = lax.dynamic_slice_in_dim(occ_irrep, NI + own_index * k_local, k_local)
    wanted = jnp.bitwise_xor(k_lab[:, None], row_lab[None, :])
    ranks = tile_ranks(tile_irrep)
    slot_ids = jnp.arange(slot_count, dtype=jnp.int32)
    select = (tile_irrep[None, None, None, :] == wanted[:, :, None, None]) & (
        ranks[None, None, None, :] == slot_ids[None, None, :, None]
    )
    pieces = regrouped.reshape(k_local, rows, slot_count, TILE)
    dense = jnp.einsum(
        "krjt,krje->krte", select.astype(jnp.bfloat16), pieces, preferred_element_type=jnp.float32
    )
    masked = dense.reshape(k_local, rows, V).astype(jnp.bfloat16)
    summed = lax.psum_scatter(
        jnp.einsum("kmc,kcn->mn", masked, integrals, preferred_element_type=jnp.float32),
        "own",
        scatter_dimension=0,
        tiled=True,
    )
    share = summed.shape[0]
    blocks = summed.reshape(share, n_amp, n_own, share)
    moved = lax.all_to_all(
        lax.all_to_all(blocks, "amp", split_axis=1, concat_axis=1, tiled=True),
        "own",
        split_axis=2,
        concat_axis=2,
        tiled=True,
    )
    mirrored = jnp.transpose(moved, (3, 1, 2, 0)).reshape(share, NI * V)
    return (summed + mirrored).astype(jnp.bfloat16)


def solution(mesh):
    return jax.shard_map(
        shards,
        mesh=mesh,
        in_specs=(P("own", None, "amp"), P("own", None, None), P(), P()),
        out_specs=P(("amp", "own"), None),
        check_vma=False,
    )
```

profile of v0, /device:TPU:0, one launch (start us, length us, event | category | flops | bytes accessed | tf_op | source)
XLA Modules:
  0.0 252.3 jit_solution(9332235532349839505)
XLA Ops:
  6.5 3.6 %copy.25 = bf16[4,2304,48]{2,0,1:T(4,128)(2,1)S(1)} copy(bf16[4,2304,48]{1,2,0:T(8,128)(2,1)} %param.4) | data formatting | bytes 1769472 | tf_op args[0]
  10.1 0.0 copy-start.1
  10.1 0.0 copy-start.2
  10.1 4.6 %reshape.80 = bf16[4,2,55296]{2,1,0:T(2,128)(2,1)} reshape(bf16[2304,4,48]{2,1,0:T(4,128)(2,1)S(1)} %bitcast.18) | data formatting | bytes 1769472
  14.8 4.2 %all-to-all-start = ((bf16[4,2,55296]{2,1,0:T(2,128)(2,1)}), bf16[4,2,55296]{2,1,0:T(2,128)(2,1)S(1)}, u32[]{:S(2)}, u32[]{:S(2)}) async-start(bf16[4,2,55296]{2,1,0:T(2,128)(2,1)} %reshape.80), calls=%async_computation | async-start | bytes 1769472 | tf_op jit(solution)/shard_map/all_to_all | solution.py:23
  19.0 0.0 reduce-scatter.2.cloned.1.call-start
  19.0 0.0 copy-done.1
  19.0 0.2 convert_reduce_fusion
  19.2 0.1 broadcast_in_dim.5
  19.3 0.1 tile.8
  19.3 0.0 copy-done.2
  19.3 0.1 dynamic_slice.6
  19.4 0.1 broadcast_xor_fusion.1
  19.5 0.1 dynamic_slice.7
  19.6 0.1 broadcast_xor_fusion
  19.7 1.1 broadcast_compare_fusion
  20.8 10.9 %all-to-all-done = bf16[4,2,55296]{2,1,0:T(2,128)(2,1)S(1)} async-done(((bf16[4,2,55296]{2,1,0:T(2,128)(2,1)}), bf16[4,2,55296]{2,1,0:T(2,128)(2,1)S(1)}, u32[]{:S(2)}, u32[]{:S(2)}) %all-to-all-start) | async-done | bytes 884768 | tf_op jit(solution)/shard_map/all_to_all | solution.py:23
  31.7 2.4 reshape.81
  34.1 1.5 copy.27
  35.6 1.5 copy.28
  37.1 11.1 %convolution_convert_fusion = bf16[4,576,18,64]{3,2,1,0:T(8,128)(2,1)} fusion(bf16[4,576,3,64]{3,2,1,0:T(4,128)(2,1)S(1)} %copy.28, pred[3,18]{1,0:T(4,128)(4,1)S(1)} %iota_compare_fusion.1, pred[4,576,18]{2,1,0:T(8,128)(4,1)} %broadcast_compare_fusion), kind=kOutput, calls=%fused_computation | convolution fusion | flops 18703872 | bytes 6234678 | tf_op jit(solution)/shard_map/krjt,krje->krte/dot_general | solution.py:37
  48.2 15.5 %copy.29 = bf16[4,576,18,64]{1,3,2,0:T(8,128)(2,1)} copy(bf16[4,576,18,64]{3,2,1,0:T(8,128)(2,1)} %convolution_convert_fusion) | data formatting | bytes 10616832 | tf_op jit(solution)/shard_map/convert_element_type | solution.py:40
  63.7 19.2 %convolution_bitcast_fusion = f32[576,2304]{1,0:T(8,128)} fusion(bf16[4,576,1152]{1,2,0:T(8,128)(2,1)} %bitcast.19, bf16[4,1152,2304]{2,1,0:T(8,128)(2,1)} %param.5), kind=kOutput, calls=%fused_computation.1 | convolution fusion | flops 12230590464 | bytes 31850496 | tf_op jit(solution)/shard_map/kmc,kcn->mn/dot_general | solution.py:42
  82.8 0.0 reduce-scatter.2.cloned.1.call-update
  82.9 105.3 %reduce-scatter.2.cloned.1.call-done = f32[72,2304]{1,0:T(8,128)} async-done(((f32[576,2304]{1,0:T(8,128)}), f32[72,2304]{1,0:T(8,128)}) %reduce-scatter.2.cloned.1.call-update) | async-done | bytes 663568 | tf_op jit(solution)/shard_map/reduce_scatter | solution.py:41
  188.2 2.3 reshape.77
  190.5 0.9 copy.31
  191.4 18.4 %all_to_all.25 = f32[72,4,8,72]{0,2,3,1:T(8,128)S(1)} all-to-all(f32[72,4,8,72]{0,2,3,1:T(8,128)S(1)} %copy.31), channel_id=1, replica_groups=mesh['amp'=4,'own'=8] {'amp'}, dimensions={1} | all-to-all | bytes 1327104 | tf_op jit(solution)/shard_map/all_to_all | solution.py:50
  209.8 0.8 copy.32
  210.6 32.7 %all_to_all.26 = f32[72,4,8,72]{0,1,3,2:T(4,128)S(1)} all-to-all(f32[72,4,8,72]{0,1,3,2:T(4,128)S(1)} %copy.32), channel_id=1, replica_groups=mesh['amp'=4,'own'=8] {'own'}, dimensions={2} | all-to-all | bytes 1327104 | tf_op jit(solution)/shard_map/all_to_all | solution.py:49
  243.3 0.0 copy-start
  243.3 0.7 copy.33
  244.0 0.6 reshape.78
  244.7 0.0 copy-done
  244.7 0.8 add_convert_fusion
  (2 shorter events, 0.0 us)
Async XLA Ops:
  10.1 8.9 %copy-start.1 = (s32[18]{0:T(128)S(1)}, s32[18]{0:T(128)}, u32[]{:S(2)}) copy-start(s32[18]{0:T(128)} %param.7) | copy-start | bytes 220
  10.1 9.2 %copy-start.2 = (s32[34]{0:T(128)S(1)}, s32[34]{0:T(128)}, u32[]{:S(2)}) copy-start(s32[34]{0:T(128)} %param.6) | copy-start | bytes 412
  14.8 16.9 %all-to-all-start = ((bf16[4,2,55296]{2,1,0:T(2,128)(2,1)}), bf16[4,2,55296]{2,1,0:T(2,128)(2,1)S(1)}, u32[]{:S(2)}, u32[]{:S(2)}) async-start(bf16[4,2,55296]{2,1,0:T(2,128)(2,1)} %reshape.80), calls=%async_computation | async-start | bytes 1769472 | tf_op jit(solution)/shard_map/all_to_all | solution.py:23
  19.0 169.2 %reduce-scatter.2.cloned.1.call-start = ((), (), s32[]{:S(2)}) async-start(), calls=%async_computation.4 | async-start | bytes 5971968 | tf_op jit(solution)/shard_map/reduce_scatter | solution.py:41
  243.3 1.3 copy-start
Sparse Core Ops, SparseCore 0:
  83.0 105.1 reduce-scatter.1
where the time goes:
time: 253 us; the launch traced here: 252 us
  waiting for transfers between devices  116 us (46%)
  blocking collectives  51.1 us (20%)
  local copies, waits for them, and re-layouts  34.7 us (14%)
  matrix products  30.3 us (12%)
  between operations  13.5 us (5%)
  starting transfers between devices  4.24 us (2%)
    reduce_scatter x1, waiting for transfers between devices, shards(): lax.psum_scatter(jnp.einsum('kmc,kcn->mn', masked, integrals, preferred_e...  105 us
    all_to_all x1, blocking collectives, shards(): lax.all_to_all(lax.all_to_all(blocks, 'amp', split_axis=1, concat_axis=1,...  32.7 us
    dot_general x1, matrix products, shards(): jnp.einsum('kmc,kcn->mn', masked, integrals, preferred_element_type=jnp.f...  19.2 us
    all_to_all x1, blocking collectives, shards(): lax.all_to_all(blocks, 'amp', split_axis=1, concat_axis=1, tiled=True)  18.4 us
    convert_element_type x1, local copies, waits for them, and re-layouts, shards(): masked = dense.reshape(k_local, rows, V).astype(jnp.bfloat16)  15.5 us
    dot_general x1, matrix products, shards(): jnp.einsum('krjt,krje->krte', select.astype(jnp.bfloat16), pieces, prefer...  11.1 us
    all_to_all x1, waiting for transfers between devices, shards(): lax.all_to_all(amplitudes, 'amp', split_axis=1, concat_axis=2, tiled=True)  10.9 us
    unnamed x9, local copies, waits for them, and re-layouts  10.6 us
  transfers between devices with their start and end apart: 2, of which 2 were waited for; matrix products, arithmetic and copies ran while one was open for 1% of the time, Pallas kernels for 0%

commit v1 on v0

--- a/solution.py
+++ b/solution.py
@@ -6,6 +6,22 @@
 V = 1152
 TILE = 64
 NI = 2
+
+
+def swapped_with_each(shard, axis, split, join):
+    ways, here = (lax.axis_size(axis), lax.axis_index(axis))
+    width = shard.shape[split] // ways
+    shape = list(shard.shape)
+    shape[split] = width
+    height = shape[join]
+    shape[join] = height * ways
+    full = jnp.zeros(shape, shard.dtype)
+    for mask in range(ways):
+        part = lax.dynamic_slice_in_dim(shard, (here ^ mask) * width, width, axis=split)
+        if mask:
+            part = lax.ppermute(part, axis, [(d, d ^ mask) for d in range(ways)])
+        full = lax.dynamic_update_slice_in_dim(full, part, (here ^ mask) * height, axis=join)
+    return full
 
 
 def tile_ranks(tile_irrep):
@@ -20,7 +36,7 @@
     own_index = lax.axis_index("own")
     n_amp = lax.axis_size("amp")
     n_own = lax.axis_size("own")
-    regrouped = lax.all_to_all(amplitudes, "amp", split_axis=1, concat_axis=2, tiled=True)
+    regrouped = swapped_with_each(amplitudes, "amp", 1, 2)
     k_local, rows, packed_width = regrouped.shape
     slot_count = packed_width // TILE
     virt_lab = jnp.repeat(tile_irrep, TILE)

time: 253 us -> 241 us (0.953)
  local copies, waits for them, and re-layouts: 34.7 us -> 24.5 us
    all_to_all x1 -> x0, waiting for transfers between devices: 10.9 us -> none  [shards(): lax.all_to_all(amplitudes, 'amp', split_axis=1, concat_axis=2, tiled=True)]
    unnamed x9 -> x6, local copies, waits for them, and re-layouts: 10.6 us -> 0.01 us
    ppermute x0 -> x3, waiting for transfers between devices: none -> 9.21 us  [swapped_with_each(): part = lax.ppermute(part, axis, [(d, d ^ mask) for d in range(ways)])]
    all_to_all x1 -> x0, starting transfers between devices: 4.24 us -> none  [shards(): lax.all_to_all(amplitudes, 'amp', split_axis=1, concat_axis=2, tiled=True)]
    ppermute x0 -> x3, starting transfers between devices: none -> 3.18 us  [swapped_with_each(): part = lax.ppermute(part, axis, [(d, d ^ mask) for d in range(ways)])]
  transfers between devices with their start and end apart: 2 -> 4, of which waited for: 2 -> 2; matrix products, arithmetic and copies ran while one was open for 1% -> 1% of each run, Pallas kernels for 0% -> 0%
where the time goes in v1:
time: 241 us; the launch traced here: 240 us
  waiting for transfers between devices  115 us (48%)
  blocking collectives  51.2 us (21%)
  matrix products  30.2 us (13%)
  local copies, waits for them, and re-layouts  24.5 us (10%)
  between operations  13.5 us (6%)
  starting transfers between devices  3.18 us (1%)
    reduce_scatter x1, waiting for transfers between devices, shards(): lax.psum_scatter(jnp.einsum('kmc,kcn->mn', masked, integrals, preferred_e...  106 us
    all_to_all x1, blocking collectives, shards(): lax.all_to_all(lax.all_to_all(blocks, 'amp', split_axis=1, concat_axis=1,...  32.7 us
    dot_general x1, matrix products, shards(): jnp.einsum('kmc,kcn->mn', masked, integrals, preferred_element_type=jnp.f...  19.1 us
    all_to_all x1, blocking collectives, shards(): lax.all_to_all(blocks, 'amp', split_axis=1, concat_axis=1, tiled=True)  18.4 us
    convert_element_type x1, local copies, waits for them, and re-layouts, shards(): masked = dense.reshape(k_local, rows, V).astype(jnp.bfloat16)  15.4 us
    dot_general x1, matrix products, shards(): jnp.einsum('krjt,krje->krte', select.astype(jnp.bfloat16), pieces, prefer...  11.1 us
    ppermute x3, waiting for transfers between devices, swapped_with_each(): part = lax.ppermute(part, axis, [(d, d ^ mask) for d in range(ways)])  9.21 us
  transfers between devices with their start and end apart: 4, of which 2 were waited for; matrix products, arithmetic and copies ran while one was open for 1% of the time, Pallas kernels for 0%

profile of v1, /device:TPU:0, one launch (start us, length us, event | category | flops | bytes accessed | tf_op | source)
XLA Modules:
  0.0 240.2 jit_solution(1655423696086155328)
XLA Ops:
  6.5 0.0 copy-start.1
  6.5 0.0 copy-start.2
  6.5 0.0 reduce-scatter.2.cloned.1.call-start
  6.5 0.1 broadcast_in_dim.8
  6.6 1.8 constant_dynamic-slice_fusion
  8.4 2.4 %collective-permute-start.2 = (bf16[4,576,48]{1,2,0:T(8,128)(2,1)S(1)}, bf16[4,576,48]{1,2,0:T(8,128)(2,1)S(1)}, u32[]{:S(2)}, u32[]{:S(2)}) collective-permute-start(bf16[4,576,48]{1,2,0:T(8,128)(2,1)S(1)} %get-tuple-element.5), channel_id=1, source_target_pairs={{0,24},{8,16},{16,8},{24,0},{1,25},{9,17},{17,9},{25,1},{2,26},{10... | collective-permute-start | bytes 663560 | tf_op jit(solution)/shard_map/ppermute | solution.py:22
  10.8 0.7 collective-permute-start
  11.5 0.0 collective-permute-start.1
  11.6 0.0 copy-done.1
  11.6 0.2 convert_reduce_fusion
  11.7 0.1 broadcast_in_dim.7
  11.8 0.1 tile.8
  11.9 0.0 copy-done.2
  11.9 0.1 dynamic_slice.18
  12.0 0.1 broadcast_xor_fusion.1
  12.1 0.1 dynamic_slice.19
  12.1 0.1 broadcast_xor_fusion
  12.2 1.1 broadcast_compare_fusion
  13.3 0.0 collective-permute-done
  13.4 9.2 %collective-permute-done.1 = bf16[4,576,48]{1,2,0:T(8,128)(2,1)S(1)} collective-permute-done((bf16[4,576,48]{1,2,0:T(8,128)(2,1)S(1)}, bf16[4,576,48]{1,2,0:T(8,128)(2,1)S(1)}, u32[]{:S(2)}, u32[]{:S(2)}) %collective-permute-start.1) | collective-permute-done | bytes 221216 | tf_op jit(solution)/shard_map/ppermute | solution.py:22
  22.6 0.0 collective-permute-done.2
  22.7 1.5 copy.20
  24.2 11.1 %convolution_convert_fusion = bf16[4,576,18,64]{3,2,1,0:T(8,128)(2,1)} fusion(bf16[4,576,3,64]{3,2,1,0:T(4,128)(2,1)S(1)} %copy.20, pred[3,18]{1,0:T(4,128)(4,1)S(1)} %iota_compare_fusion.1, pred[4,576,18]{2,1,0:T(8,128)(4,1)} %broadcast_compare_fusion), kind=kOutput, calls=%fused_computation | convolution fusion | flops 18703872 | bytes 6234678 | tf_op jit(solution)/shard_map/krjt,krje->krte/dot_general | solution.py:53
  35.3 15.4 %copy.21 = bf16[4,576,18,64]{1,3,2,0:T(8,128)(2,1)} copy(bf16[4,576,18,64]{3,2,1,0:T(8,128)(2,1)} %convolution_convert_fusion) | data formatting | bytes 10616832 | tf_op jit(solution)/shard_map/convert_element_type | solution.py:56
  50.7 19.1 %convolution_bitcast_fusion = f32[576,2304]{1,0:T(8,128)} fusion(bf16[4,576,1152]{1,2,0:T(8,128)(2,1)} %bitcast.11, bf16[4,1152,2304]{2,1,0:T(8,128)(2,1)} %param.5), kind=kOutput, calls=%fused_computation.1 | convolution fusion | flops 12230590464 | bytes 31850496 | tf_op jit(solution)/shard_map/kmc,kcn->mn/dot_general | solution.py:58
  69.8 0.0 reduce-scatter.2.cloned.1.call-update
  69.8 106.2 %reduce-scatter.2.cloned.1.call-done = f32[72,2304]{1,0:T(8,128)} async-done(((f32[576,2304]{1,0:T(8,128)}), f32[72,2304]{1,0:T(8,128)}) %reduce-scatter.2.cloned.1.call-update) | async-done | bytes 663568 | tf_op jit(solution)/shard_map/reduce_scatter | solution.py:57
  176.1 2.3 reshape.76
  178.4 0.9 copy.23
  179.3 18.4 %all_to_all.10 = f32[72,4,8,72]{0,2,3,1:T(8,128)S(1)} all-to-all(f32[72,4,8,72]{0,2,3,1:T(8,128)S(1)} %copy.23), channel_id=1, replica_groups=mesh['amp'=4,'own'=8] {'amp'}, dimensions={1} | all-to-all | bytes 1327104 | tf_op jit(solution)/shard_map/all_to_all | solution.py:66
  197.8 0.8 copy.24
  198.5 32.7 %all_to_all.11 = f32[72,4,8,72]{0,1,3,2:T(4,128)S(1)} all-to-all(f32[72,4,8,72]{0,1,3,2:T(4,128)S(1)} %copy.24), channel_id=1, replica_groups=mesh['amp'=4,'own'=8] {'own'}, dimensions={2} | all-to-all | bytes 1327104 | tf_op jit(solution)/shard_map/all_to_all | solution.py:65
  231.3 0.0 copy-start
  231.3 0.7 copy.25
  231.9 0.6 reshape.77
  232.6 0.0 copy-done
  232.6 0.8 add_convert_fusion
  (5 shorter events, 0.1 us)
Async XLA Ops:
  6.5 5.0 %copy-start.1 = (s32[18]{0:T(128)S(1)}, s32[18]{0:T(128)}, u32[]{:S(2)}) copy-start(s32[18]{0:T(128)} %param.7) | copy-start | bytes 220
  6.5 5.4 %copy-start.2 = (s32[34]{0:T(128)S(1)}, s32[34]{0:T(128)}, u32[]{:S(2)}) copy-start(s32[34]{0:T(128)} %param.6) | copy-start | bytes 412
  6.5 169.5 %reduce-scatter.2.cloned.1.call-start = ((), (), s32[]{:S(2)}) async-start(), calls=%async_computation.3 | async-start | bytes 5971968 | tf_op jit(solution)/shard_map/reduce_scatter | solution.py:57
  8.4 14.3 %collective-permute-start.2 = (bf16[4,576,48]{1,2,0:T(8,128)(2,1)S(1)}, bf16[4,576,48]{1,2,0:T(8,128)(2,1)S(1)}, u32[]{:S(2)}, u32[]{:S(2)}) collective-permute-start(bf16[4,576,48]{1,2,0:T(8,128)(2,1)S(1)} %get-tuple-element.5), channel_id=1, source_target_pairs={{0,24},{8,16},{16,8},{24,0},{1,25},{9,17},{17,9},{25,1},{2,26},{10... | collective-permute-start | bytes 663560 | tf_op jit(solution)/shard_map/ppermute | solution.py:22
  10.8 2.5 %collective-permute-start = (bf16[4,576,48]{1,2,0:T(8,128)(2,1)S(1)}, bf16[4,576,48]{1,2,0:T(8,128)(2,1)S(1)}, u32[]{:S(2)}, u32[]{:S(2)}) collective-permute-start(bf16[4,576,48]{1,2,0:T(8,128)(2,1)S(1)} %get-tuple-element.6), channel_id=1, source_target_pairs={{0,8},{8,0},{16,24},{24,16},{1,9},{9,1},{17,25},{25,17},{2,10},{10... | collective-permute-start | bytes 663560 | tf_op jit(solution)/shard_map/ppermute | solution.py:22
  11.5 11.1 %collective-permute-start.1 = (bf16[4,576,48]{1,2,0:T(8,128)(2,1)S(1)}, bf16[4,576,48]{1,2,0:T(8,128)(2,1)S(1)}, u32[]{:S(2)}, u32[]{:S(2)}) collective-permute-start(bf16[4,576,48]{1,2,0:T(8,128)(2,1)S(1)} %get-tuple-element.8), channel_id=1, source_target_pairs={{0,16},{8,24},{16,0},{24,8},{1,17},{9,25},{17,1},{25,9},{2,18},{10... | collective-permute-start | bytes 663560 | tf_op jit(solution)/shard_map/ppermute | solution.py:22
  231.3 1.3 copy-start
Sparse Core Ops, SparseCore 0:
  70.0 106.0 reduce-scatter.1
